TPU v7x, 32 devices: a whole 2x2x4 slice. The times are simulated.
32 devices in a mesh: gx: 8 (over y, x, core), gy: 4 (over z).
Axes of the slice: x: 2, y: 2, z: 4, core: 2. Of those that a mesh axis runs over, the one named last changes fastest.
Arguments:
- positions: float32 [3, 8, 4, 32, 128], P(None, 'gx', 'gy'), may hold values from 0 to 1023, as said below
- counts: int32 [8, 4, 32], P('gx', 'gy'), may hold values from 16 to 128, as said below
- labels: int32 [8, 4, 32, 128], P('gx', 'gy'), may hold values from 0 to 5592404
Outputs:
- groups: int32 [8, 4, 32, 128], P('gx', 'gy')
Inputs may be any that keep to these rules, and one draw needn't show every extreme that they name: `positions`: coordinates are whole numbers. `counts`: at least one cell holds 128 particles; slots at or beyond a cell's count are padding.
All inputs are finite; a program needn't handle non-finite values.
Results may differ from a plain program's by a relative error of at most 0.000001.
Values sent between devices are 32-bit elements; how exact they have to be, the bound alone decides.
A program may use at most 64 MiB of HBM per device.

v0:
```python
import itertools

import jax
import jax.numpy as jnp
from jax import lax
from jax.experimental import pallas as pl
from jax.experimental.pallas import tpu as pltpu
from jax.sharding import PartitionSpec as P

ITERS = 3

cell_side = 1024.0
link_square = 1040.0
sentinel = 16777216.0
middle = 512.0
reach = 64.0
step_row = 16
own_row = 24

MESH = pl.DeviceIdType.MESH

SUBSETS = [s for s in itertools.product((0, 1), repeat=3) if any(s)]
SUBSETS.sort(key=sum)
SIDES = {
    subset: list(itertools.product(*[(-1, 1) if crossed else (0,) for crossed in subset])) for subset in SUBSETS
}
BLOCKS = [sides for subset in SUBSETS for sides in SIDES[subset]]
COLUMNS = [c for c in itertools.product((-1, 0, 1), repeat=2) if c != (0, 0)]


def thirds(value):
    top = jnp.floor(value * (1.0 / 65536.0)) * 65536.0
    rest = value - top
    mid = jnp.floor(rest * (1.0 / 256.0)) * 256.0
    return [top, mid, rest - mid]


def halves(value):
    high = jnp.floor(value * (1.0 / 32.0)) * 32.0
    return high, value - high


def near_rows(points, sides):
    terms, norm = [], None
    for value, side in zip(points, sides):
        if side == 0:
            value = value - middle
            high, low = halves(value)
            terms += [high, low, high, low]
        else:
            value = jnp.minimum(value, reach) if side > 0 else jnp.maximum(value - cell_side, -reach)
            terms += [value]
        norm = value * value if norm is None else norm + value * value
    one = jnp.ones_like(norm)
    return thirds(norm) + [one, one, one] + terms


def own_rows(points, sides):
    terms, norm, chosen = [], None, None
    for value, side in zip(points, sides):
        if side == 0:
            value = value - middle
            high, low = halves(value)
            terms += [-2.0 * high, -2.0 * high, -2.0 * low, -2.0 * low]
        else:
            here = value >= middle if side > 0 else value < middle
            chosen = here if chosen is None else jnp.logical_and(chosen, here)
            value = jnp.maximum(value - cell_side, -reach) if side > 0 else jnp.minimum(value, reach)
            terms += [-2.0 * value]
        norm = value * value if norm is None else norm + value * value
    one = jnp.ones_like(norm)
    rows = [one, one, one] + thirds(norm - link_square) + terms
    scale = sentinel if chosen is None else jnp.where(chosen, sentinel, 0.0)
    return [row * scale for row in rows]


def put_rows(ref, rows, depth, size):
    zero = jnp.zeros_like(rows[0])
    for k in range(size):
        ref[pl.ds(k, depth, stride=size), :] = rows[k] if k < len(rows) else zero


def kernel(
    counts_ref, points_ref, labels_ref, groups_ref,
    halo_points, halo_labels, current, own_a, own_b, far_a, far_b, near_labels,
    turned0, turned1, turned2, turned3, gap,
    point_send, point_recv, label_send, label_recv,
):
    _, depth, slots = points_ref.shape
    gx, gy = lax.axis_size("gx"), lax.axis_size("gy")
    me_x, me_y = lax.axis_index("gx"), lax.axis_index("gy")

    def target(offset):
        return (lax.rem(me_x - offset[0] + gx, gx), lax.rem(me_y - offset[1] + gy, gy))

    barrier = pltpu.get_barrier_semaphore()
    for offset in COLUMNS:
        pl.semaphore_signal(barrier, inc=1, device_id=target(offset), device_id_type=MESH)

    slot = lax.broadcasted_iota(jnp.int32, (1, slots), 1)
    for e in range(depth):
        here = labels_ref[e : e + 1, :].astype(jnp.float32)
        current[0, e : e + 1, :] = jnp.where(slot < counts_ref[e], here, sentinel)

    pl.semaphore_wait(barrier, len(COLUMNS))

    def label_copies(step):
        return [
            pltpu.make_async_remote_copy(
                src_ref=current.at[step],
                dst_ref=halo_labels.at[step, n],
                send_sem=label_send.at[step, n],
                recv_sem=label_recv.at[step, n],
                device_id=target(offset),
                device_id_type=MESH,
            )
            for n, offset in enumerate(COLUMNS)
        ]

    point_copies = [
        pltpu.make_async_remote_copy(
            src_ref=points_ref,
            dst_ref=halo_points.at[n],
            send_sem=point_send.at[n],
            recv_sem=point_recv.at[n],
            device_id=target(offset),
            device_id_type=MESH,
        )
        for n, offset in enumerate(COLUMNS)
    ]
    for copy in point_copies:
        copy.start()
    copies = label_copies(0)
    for copy in copies:
        copy.start()

    own_points = [points_ref[k] for k in range(3)]
    put_rows(own_a, own_rows(own_points, (0, 0, 0)), depth, own_row)
    put_rows(own_b, near_rows(own_points, (0, 0, 0)), depth, own_row)
    for n, sides in enumerate(BLOCKS):
        put_rows(far_a.at[n], own_rows(own_points, sides), depth, step_row)
        if sides[:2] == (0, 0):
            put_rows(far_b.at[n], near_rows(own_points, sides), depth, step_row)

    turned = {1: turned1, 2: turned2, 3: turned3}
    place = {}
    for subset in SUBSETS:
        place[subset] = sum(1 for other in place if sum(other) == sum(subset))

    @pl.loop(0, depth)
    def _(e):
        at = pl.multiple_of(e * own_row, 8)
        turned0[e] = own_a[pl.ds(at, own_row), :].T.astype(jnp.bfloat16)
        at = pl.multiple_of(e * step_row, step_row)
        for subset in SUBSETS:
            rows = [far_a[BLOCKS.index(sides), pl.ds(at, step_row), :] for sides in SIDES[subset]]
            turned[sum(subset)][place[subset], e] = jnp.concatenate(rows, axis=0).T.astype(jnp.bfloat16)

    def put_labels(n, value):
        for k, row in enumerate(thirds(value)):
            near_labels[n, pl.ds(k, depth, stride=step_row), :] = row * (1.0 / sentinel)

    near_labels[...] = jnp.zeros_like(near_labels)

    for copy in point_copies:
        copy.wait_recv()
    for n, offset in enumerate(COLUMNS):
        points = [halo_points[n, k] for k in range(3)]
        for m, sides in enumerate(BLOCKS):
            if sides[:2] == offset:
                put_rows(far_b.at[m], near_rows(points, sides), depth, step_row)

    for step in range(ITERS):
        if step > 0:
            copies = label_copies(step)
            for copy in copies:
                copy.start()
        put_labels(len(COLUMNS), current[step])
        for copy in copies:
            copy.wait_recv()
        for n in range(len(COLUMNS)):
            put_labels(n, halo_labels[step, n])

        @pl.loop(0, depth)
        def _(e):
            spots = {
                0: pl.multiple_of(e * step_row, step_row),
                1: pl.multiple_of(lax.rem(e + 1, depth) * step_row, step_row),
                -1: pl.multiple_of(lax.rem(e + depth - 1, depth) * step_row, step_row),
            }
            own = current[step, pl.ds(e, 1), :]
            if step == 0:
                at = pl.multiple_of(e * own_row, 8)
                found = jnp.dot(
                    turned0[e],
                    own_b[pl.ds(at, own_row), :].astype(jnp.bfloat16),
                    preferred_element_type=jnp.float32,
                )
                gap[e, 0] = found
            else:
                found = gap[e, 0]
            least = jnp.maximum(found, own)
            for m, subset in enumerate(SUBSETS):
                sides_list = SIDES[subset]
                left = turned[sum(subset)][place[subset], e]
                columns = [COLUMNS.index(s[:2]) if s[:2] != (0, 0) else len(COLUMNS) for s in sides_list]
                right = jnp.concatenate(
                    [near_labels[c, pl.ds(spots[s[2]], step_row), :] for c, s in zip(columns, sides_list)], axis=0
                )
                if step == 0:
                    front = jnp.concatenate(
                        [far_b[BLOCKS.index(s), pl.ds(spots[s[2]], step_row), :] for s in sides_list], axis=0
                    )
                    both = jnp.concatenate([front, right], axis=1).astype(jnp.bfloat16)
                    result = jnp.dot(left, both, preferred_element_type=jnp.float32)
                    found, values = result[:, :slots], result[:, slots:]
                    gap[e, m + 1] = found
                else:
                    values = jnp.dot(left, right.astype(jnp.bfloat16), preferred_element_type=jnp.float32)
                    found = gap[e, m + 1]
                least = jnp.minimum(least, jnp.maximum(found, values))
            row = jnp.minimum(jnp.min(least.T, axis=0, keepdims=True), own)
            filled = slot < counts_ref[e]
            if step == ITERS - 1:
                groups_ref[pl.ds(e, 1), :] = jnp.where(filled, row, -1.0).astype(jnp.int32)
            else:
                current[step + 1, pl.ds(e, 1), :] = jnp.where(filled, row, sentinel)

        for copy in copies:
            copy.wait_send()
    for copy in point_copies:
        copy.wait_send()


def body(positions, counts, labels):
    depth, slots = positions.shape[3:]
    near = len(COLUMNS)
    groups = pl.pallas_call(
        kernel,
        out_shape=jax.ShapeDtypeStruct((depth, slots), jnp.int32),
        in_specs=[
            pl.BlockSpec(memory_space=pltpu.SMEM),
            pl.BlockSpec(memory_space=pltpu.VMEM),
            pl.BlockSpec(memory_space=pltpu.VMEM),
        ],
        out_specs=pl.BlockSpec(memory_space=pltpu.VMEM),
        scratch_shapes=[
            pltpu.VMEM((near, 3, depth, slots), jnp.float32),
            pltpu.VMEM((ITERS, near, depth, slots), jnp.float32),
            pltpu.VMEM((ITERS, depth, slots), jnp.float32),
            pltpu.VMEM((depth * own_row, slots), jnp.float32),
            pltpu.VMEM((depth * own_row, slots), jnp.float32),
            pltpu.VMEM((len(BLOCKS), depth * step_row, slots), jnp.float32),
            pltpu.VMEM((len(BLOCKS), depth * step_row, slots), jnp.float32),
            pltpu.VMEM((near + 1, depth * step_row, slots), jnp.float32),
            pltpu.VMEM((depth, slots, own_row), jnp.bfloat16),
            pltpu.VMEM((3, depth, slots, 2 * step_row), jnp.bfloat16),
            pltpu.VMEM((3, depth, slots, 4 * step_row), jnp.bfloat16),
            pltpu.VMEM((1, depth, slots, 8 * step_row), jnp.bfloat16),
            pltpu.VMEM((depth, len(SUBSETS) + 1, slots, slots), jnp.float32),
            pltpu.SemaphoreType.DMA((near,)),
            pltpu.SemaphoreType.DMA((near,)),
            pltpu.SemaphoreType.DMA((ITERS, near)),
            pltpu.SemaphoreType.DMA((ITERS, near)),
        ],
        compiler_params=pltpu.CompilerParams(
            collective_id=0, has_side_effects=True, vmem_limit_bytes=60 * 2**20
        ),
    )(counts.reshape(depth), positions.reshape(3, depth, slots), labels.reshape(depth, slots))
    return groups.reshape(labels.shape)


def solution(mesh):
    placed = (P(None, "gx", "gy", None, None), P("gx", "gy", None), P("gx", "gy", None, None))
    return jax.shard_map(
        body, mesh=mesh, in_specs=placed, out_specs=P("gx", "gy", None, None), check_vma=False
    )
```

profile of v0, /device:TPU:0, one launch (start us, length us, event | category | flops | bytes accessed | tf_op | source)
XLA Modules:
  0.0 61.4 jit_solution(15261572531581043925)
XLA Ops:
  0.0 60.1 %shard_map.37 = s32[32,128]{1,0:T(8,128)} custom-call(s32[32]{0:T(128)} %bitcast.7, f32[3,32,128]{2,1,0:T(8,128)} %bitcast.5, s32[32,128]{1,0:T(8,128)} %bitcast.6), custom_call_target="tpu_custom_call" | custom-call | tf_op jit(solution)/shard_map/pallas_call | solution.py:238
  60.1 1.3 %copy.5 = s32[1,1,32,128]{3,2,1,0:T(8,128)} copy(s32[1,1,32,128]{3,2,1,0:T(8,128)} %bitcast.4) | data formatting | bytes 32768
where the time goes:
time: 61.7 us; the launch traced here: 61.4 us
  Pallas kernels  60.1 us (97%)
  local copies, waits for them, and re-layouts  1.32 us (2%)
    pallas_call x1, Pallas kernels, body(): pl.pallas_call(kernel, out_shape=jax.ShapeDtypeStruct((depth, slots), jnp...  60.1 us
    unnamed x1, local copies, waits for them, and re-layouts  1.32 us

commit v1 on v0

--- a/solution.py
+++ b/solution.py
@@ -26,6 +26,7 @@
 }
 BLOCKS = [sides for subset in SUBSETS for sides in SIDES[subset]]
 COLUMNS = [c for c in itertools.product((-1, 0, 1), repeat=2) if c != (0, 0)]
+COLUMNS.sort(key=lambda c: c[0] * c[0] + c[1] * c[1])
 
 
 def thirds(value):
@@ -38,6 +39,10 @@
 def halves(value):
     high = jnp.floor(value * (1.0 / 32.0)) * 32.0
     return high, value - high
+
+
+def block_size(crossed):
+    return 8 if crossed == 3 else step_row
 
 
 def near_rows(points, sides):
@@ -51,38 +56,60 @@
             value = jnp.minimum(value, reach) if side > 0 else jnp.maximum(value - cell_side, -reach)
             terms += [value]
         norm = value * value if norm is None else norm + value * value
-    one = jnp.ones_like(norm)
-    return thirds(norm) + [one, one, one] + terms
-
-
-def own_rows(points, sides):
-    terms, norm, chosen = [], None, None
-    for value, side in zip(points, sides):
-        if side == 0:
+    crossed = sum(abs(side) for side in sides)
+    ones = 2 if crossed == 3 else 3
+    rows = dict(enumerate(thirds(norm)))
+    if crossed == 3:
+        del rows[0]
+    rows.update((3 + ones + k, term) for k, term in enumerate(terms))
+    return rows
+
+
+def fixed_rows(sides, size, like):
+    crossed = sum(abs(side) for side in sides)
+    ones = 2 if crossed == 3 else 3
+    terms = 3 + ones + sum(1 if side else 4 for side in sides)
+    one, zero = jnp.ones_like(like), jnp.zeros_like(like)
+    rows = {3 + k: one for k in range(ones)}
+    rows.update((k, zero) for k in range(terms, size))
+    if crossed == 3:
+        rows[0] = zero
+    return rows
+
+
+def own_rows(points, subset, size):
+    terms, norm = [], None
+    for value, crossed in zip(points, subset):
+        if crossed:
+            value = jnp.where(
+                value >= middle, jnp.maximum(value - cell_side, -reach), jnp.minimum(value, reach)
+            )
+            terms += [-2.0 * value]
+        else:
             value = value - middle
             high, low = halves(value)
             terms += [-2.0 * high, -2.0 * high, -2.0 * low, -2.0 * low]
-        else:
-            here = value >= middle if side > 0 else value < middle
-            chosen = here if chosen is None else jnp.logical_and(chosen, here)
-            value = jnp.maximum(value - cell_side, -reach) if side > 0 else jnp.minimum(value, reach)
-            terms += [-2.0 * value]
         norm = value * value if norm is None else norm + value * value
     one = jnp.ones_like(norm)
-    rows = [one, one, one] + thirds(norm - link_square) + terms
-    scale = sentinel if chosen is None else jnp.where(chosen, sentinel, 0.0)
-    return [row * scale for row in rows]
+    norm = norm - link_square
+    if sum(subset) == 3:
+        mid = jnp.floor(norm * (1.0 / 256.0)) * 256.0
+        split = [mid, norm - mid]
+    else:
+        split = thirds(norm)
+    rows = [one, one, one] + split + terms
+    rows += [jnp.zeros_like(norm)] * (size - len(rows))
+    return dict(enumerate(rows))
 
 
 def put_rows(ref, rows, depth, size):
-    zero = jnp.zeros_like(rows[0])
-    for k in range(size):
-        ref[pl.ds(k, depth, stride=size), :] = rows[k] if k < len(rows) else zero
+    for k, row in rows.items():
+        ref[pl.ds(k, depth, stride=size), :] = row
 
 
 def kernel(
     counts_ref, points_ref, labels_ref, groups_ref,
-    halo_points, halo_labels, current, own_a, own_b, far_a, far_b, near_labels,
+    halo_points, halo_labels, current, own_a, own_b, side_a, hot, far_b, corner_b, near_labels,
     turned0, turned1, turned2, turned3, gap,
     point_send, point_recv, label_send, label_recv,
 ):
@@ -135,26 +162,47 @@
         copy.start()
 
     own_points = [points_ref[k] for k in range(3)]
-    put_rows(own_a, own_rows(own_points, (0, 0, 0)), depth, own_row)
-    put_rows(own_b, near_rows(own_points, (0, 0, 0)), depth, own_row)
+
+    def near_block(sides):
+        if all(sides):
+            return corner_b.at[BLOCKS.index(sides) - len(BLOCKS) + 8]
+        return far_b.at[BLOCKS.index(sides)]
+
+    put_rows(own_a, own_rows(own_points, (0, 0, 0), own_row), depth, own_row)
+    for m, subset in enumerate(SUBSETS):
+        put_rows(side_a.at[m], own_rows(own_points, subset, block_size(sum(subset))), depth, block_size(sum(subset)))
+    upper = [value >= middle for value in own_points]
     for n, sides in enumerate(BLOCKS):
-        put_rows(far_a.at[n], own_rows(own_points, sides), depth, step_row)
-        if sides[:2] == (0, 0):
-            put_rows(far_b.at[n], near_rows(own_points, sides), depth, step_row)
+        chosen = None
+        for high, side in zip(upper, sides):
+            if side:
+                here = high if side > 0 else jnp.logical_not(high)
+                chosen = here if chosen is None else jnp.logical_and(chosen, here)
+        hot[n] = jnp.where(chosen, sentinel, 0.0)
 
     turned = {1: turned1, 2: turned2, 3: turned3}
     place = {}
     for subset in SUBSETS:
         place[subset] = sum(1 for other in place if sum(other) == sum(subset))
 
-    @pl.loop(0, depth)
+    @pl.loop(0, depth, unroll=2)
     def _(e):
         at = pl.multiple_of(e * own_row, 8)
-        turned0[e] = own_a[pl.ds(at, own_row), :].T.astype(jnp.bfloat16)
-        at = pl.multiple_of(e * step_row, step_row)
-        for subset in SUBSETS:
-            rows = [far_a[BLOCKS.index(sides), pl.ds(at, step_row), :] for sides in SIDES[subset]]
+        turned0[e] = (own_a[pl.ds(at, own_row), :] * sentinel).T.astype(jnp.bfloat16)
+        for m, subset in enumerate(SUBSETS):
+            size = block_size(sum(subset))
+            base = side_a[m, pl.ds(pl.multiple_of(e * size, size), size), :]
+            rows = [base * hot[BLOCKS.index(sides), pl.ds(e, 1), :] for sides in SIDES[subset]]
             turned[sum(subset)][place[subset], e] = jnp.concatenate(rows, axis=0).T.astype(jnp.bfloat16)
+
+    like = own_points[0]
+    put_rows(own_b, fixed_rows((0, 0, 0), own_row, like), depth, own_row)
+    put_rows(own_b, near_rows(own_points, (0, 0, 0)), depth, own_row)
+    for sides in BLOCKS:
+        size = block_size(sum(abs(side) for side in sides))
+        put_rows(near_block(sides), fixed_rows(sides, size, like), depth, size)
+        if sides[:2] == (0, 0):
+            put_rows(near_block(sides), near_rows(own_points, sides), depth, size)
 
     def put_labels(n, value):
         for k, row in enumerate(thirds(value)):
@@ -162,13 +210,13 @@
 
     near_labels[...] = jnp.zeros_like(near_labels)
 
-    for copy in point_copies:
-        copy.wait_recv()
     for n, offset in enumerate(COLUMNS):
+        point_copies[n].wait_recv()
         points = [halo_points[n, k] for k in range(3)]
-        for m, sides in enumerate(BLOCKS):
+        for sides in BLOCKS:
             if sides[:2] == offset:
-                put_rows(far_b.at[m], near_rows(points, sides), depth, step_row)
+                size = block_size(sum(abs(side) for side in sides))
+                put_rows(near_block(sides), near_rows(points, sides), depth, size)
 
     for step in range(ITERS):
         if step > 0:
@@ -181,13 +229,13 @@
         for n in range(len(COLUMNS)):
             put_labels(n, halo_labels[step, n])
 
-        @pl.loop(0, depth)
+        @pl.loop(0, depth, unroll=2)
         def _(e):
-            spots = {
-                0: pl.multiple_of(e * step_row, step_row),
-                1: pl.multiple_of(lax.rem(e + 1, depth) * step_row, step_row),
-                -1: pl.multiple_of(lax.rem(e + depth - 1, depth) * step_row, step_row),
-            }
+            cells = {0: e, 1: lax.rem(e + 1, depth), -1: lax.rem(e + depth - 1, depth)}
+
+            def spot(side, stride, size):
+                return pl.ds(pl.multiple_of(cells[side] * stride, size), size)
+
             own = current[step, pl.ds(e, 1), :]
             if step == 0:
                 at = pl.multiple_of(e * own_row, 8)
@@ -204,12 +252,13 @@
                 sides_list = SIDES[subset]
                 left = turned[sum(subset)][place[subset], e]
                 columns = [COLUMNS.index(s[:2]) if s[:2] != (0, 0) else len(COLUMNS) for s in sides_list]
+                size = block_size(sum(subset))
                 right = jnp.concatenate(
-                    [near_labels[c, pl.ds(spots[s[2]], step_row), :] for c, s in zip(columns, sides_list)], axis=0
+                    [near_labels[c, spot(s[2], step_row, size), :] for c, s in zip(columns, sides_list)], axis=0
                 )
                 if step == 0:
                     front = jnp.concatenate(
-                        [far_b[BLOCKS.index(s), pl.ds(spots[s[2]], step_row), :] for s in sides_list], axis=0
+                        [near_block(s)[spot(s[2], size, size), :] for s in sides_list], axis=0
                     )
                     both = jnp.concatenate([front, right], axis=1).astype(jnp.bfloat16)
                     result = jnp.dot(left, both, preferred_element_type=jnp.float32)
@@ -250,13 +299,15 @@
             pltpu.VMEM((ITERS, depth, slots), jnp.float32),
             pltpu.VMEM((depth * own_row, slots), jnp.float32),
             pltpu.VMEM((depth * own_row, slots), jnp.float32),
-            pltpu.VMEM((len(BLOCKS), depth * step_row, slots), jnp.float32),
-            pltpu.VMEM((len(BLOCKS), depth * step_row, slots), jnp.float32),
+            pltpu.VMEM((len(SUBSETS), depth * step_row, slots), jnp.float32),
+            pltpu.VMEM((len(BLOCKS), depth, slots), jnp.float32),
+            pltpu.VMEM((len(BLOCKS) - 8, depth * step_row, slots), jnp.float32),
+            pltpu.VMEM((8, depth * 8, slots), jnp.float32),
             pltpu.VMEM((near + 1, depth * step_row, slots), jnp.float32),
             pltpu.VMEM((depth, slots, own_row), jnp.bfloat16),
             pltpu.VMEM((3, depth, slots, 2 * step_row), jnp.bfloat16),
             pltpu.VMEM((3, depth, slots, 4 * step_row), jnp.bfloat16),
-            pltpu.VMEM((1, depth, slots, 8 * step_row), jnp.bfloat16),
+            pltpu.VMEM((1, depth, slots, 8 * 8), jnp.bfloat16),
             pltpu.VMEM((depth, len(SUBSETS) + 1, slots, slots), jnp.float32),
             pltpu.SemaphoreType.DMA((near,)),
             pltpu.SemaphoreType.DMA((near,)),

time: 61.7 us -> 49.9 us (0.81)
  the two profiles are of different devices: /device:TPU:0 before, /device:TPU:1 now
where the time goes in v1:
time: 49.9 us; the launch traced here: 49.6 us
  Pallas kernels  48.3 us (97%)
  local copies, waits for them, and re-layouts  1.32 us (3%)
    pallas_call x1, Pallas kernels, body(): pl.pallas_call(kernel, out_shape=jax.ShapeDtypeStruct((depth, slots), jnp...  48.3 us
    unnamed x1, local copies, waits for them, and re-layouts  1.32 us

profile of v1, /device:TPU:1, one launch (start us, length us, event | category | flops | bytes accessed | tf_op | source)
XLA Modules:
  0.0 49.6 jit_solution(11970388754024087897)
XLA Ops:
  0.0 48.3 %shard_map.37 = s32[32,128]{1,0:T(8,128)} custom-call(s32[32]{0:T(128)} %bitcast.7, f32[3,32,128]{2,1,0:T(8,128)} %bitcast.5, s32[32,128]{1,0:T(8,128)} %bitcast.6), custom_call_target="tpu_custom_call" | custom-call | tf_op jit(solution)/shard_map/pallas_call | solution.py:287
  48.3 1.3 %copy.5 = s32[1,1,32,128]{3,2,1,0:T(8,128)} copy(s32[1,1,32,128]{3,2,1,0:T(8,128)} %bitcast.4) | data formatting | bytes 32768

commit v2 on v1

--- a/solution.py
+++ b/solution.py
@@ -15,7 +15,7 @@
 middle = 512.0
 reach = 64.0
 step_row = 16
-own_row = 24
+own_row = 32
 
 MESH = pl.DeviceIdType.MESH
 
@@ -25,8 +25,14 @@
     subset: list(itertools.product(*[(-1, 1) if crossed else (0,) for crossed in subset])) for subset in SUBSETS
 }
 BLOCKS = [sides for subset in SUBSETS for sides in SIDES[subset]]
-COLUMNS = [c for c in itertools.product((-1, 0, 1), repeat=2) if c != (0, 0)]
-COLUMNS.sort(key=lambda c: c[0] * c[0] + c[1] * c[1])
+COLUMNS = [(-1, 0), (1, 0), (0, -1), (0, 1), (-1, -1), (-1, 1), (1, -1), (1, 1)]
+
+PHASES = [
+    (((0, 0, 0), (0, 0, 1)), ()),
+    (((1, 0, 0), (1, 0, 1)), (0, 1)),
+    (((0, 1, 0), (0, 1, 1)), (2, 3)),
+    (((1, 1, 0), (1, 1, 1)), (4, 5, 6, 7)),
+]
 
 
 def thirds(value):
@@ -110,7 +116,7 @@
 def kernel(
     counts_ref, points_ref, labels_ref, groups_ref,
     halo_points, halo_labels, current, own_a, own_b, side_a, hot, far_b, corner_b, near_labels,
-    turned0, turned1, turned2, turned3, gap,
+    turned0, turned1, turned2, turned3, gap, lowest,
     point_send, point_recv, label_send, label_recv,
 ):
     _, depth, slots = points_ref.shape
@@ -155,11 +161,10 @@
         )
         for n, offset in enumerate(COLUMNS)
     ]
-    for copy in point_copies:
-        copy.start()
     copies = label_copies(0)
-    for copy in copies:
-        copy.start()
+    for point_copy, label_copy in zip(point_copies, copies):
+        point_copy.start()
+        label_copy.start()
 
     own_points = [points_ref[k] for k in range(3)]
 
@@ -180,20 +185,20 @@
                 chosen = here if chosen is None else jnp.logical_and(chosen, here)
         hot[n] = jnp.where(chosen, sentinel, 0.0)
 
-    turned = {1: turned1, 2: turned2, 3: turned3}
-    place = {}
-    for subset in SUBSETS:
-        place[subset] = sum(1 for other in place if sum(other) == sum(subset))
+    turned = (turned0, turned1, turned2, turned3)
 
     @pl.loop(0, depth, unroll=2)
     def _(e):
-        at = pl.multiple_of(e * own_row, 8)
-        turned0[e] = (own_a[pl.ds(at, own_row), :] * sentinel).T.astype(jnp.bfloat16)
-        for m, subset in enumerate(SUBSETS):
-            size = block_size(sum(subset))
-            base = side_a[m, pl.ds(pl.multiple_of(e * size, size), size), :]
-            rows = [base * hot[BLOCKS.index(sides), pl.ds(e, 1), :] for sides in SIDES[subset]]
-            turned[sum(subset)][place[subset], e] = jnp.concatenate(rows, axis=0).T.astype(jnp.bfloat16)
+        for phase, (subsets, _) in enumerate(PHASES):
+            rows = []
+            for subset in subsets:
+                if not any(subset):
+                    rows.append(own_a[pl.ds(pl.multiple_of(e * own_row, own_row), own_row), :] * sentinel)
+                    continue
+                size = block_size(sum(subset))
+                base = side_a[SUBSETS.index(subset), pl.ds(pl.multiple_of(e * size, size), size), :]
+                rows += [base * hot[BLOCKS.index(sides), pl.ds(e, 1), :] for sides in SIDES[subset]]
+            turned[phase][e] = jnp.concatenate(rows, axis=0).T.astype(jnp.bfloat16)
 
     like = own_points[0]
     put_rows(own_b, fixed_rows((0, 0, 0), own_row, like), depth, own_row)
@@ -210,13 +215,60 @@
 
     near_labels[...] = jnp.zeros_like(near_labels)
 
-    for n, offset in enumerate(COLUMNS):
-        point_copies[n].wait_recv()
-        points = [halo_points[n, k] for k in range(3)]
-        for sides in BLOCKS:
-            if sides[:2] == offset:
-                size = block_size(sum(abs(side) for side in sides))
-                put_rows(near_block(sides), near_rows(points, sides), depth, size)
+    def diagonal(first, second):
+        top = jnp.concatenate([first, jnp.zeros((first.shape[0], second.shape[1]), first.dtype)], axis=1)
+        low = jnp.concatenate([jnp.zeros((second.shape[0], first.shape[1]), first.dtype), second], axis=1)
+        return jnp.concatenate([top, low], axis=0)
+
+    def sweep(step, phase, subsets):
+        last = phase == len(PHASES) - 1
+
+        @pl.loop(0, depth, unroll=4)
+        def _(e):
+            cells = {0: e, 1: lax.rem(e + 1, depth), -1: lax.rem(e + depth - 1, depth)}
+
+            def spot(side, stride, size):
+                return pl.ds(pl.multiple_of(cells[side] * stride, size), size)
+
+            def label_rows(subset):
+                rows = []
+                for sides in SIDES[subset]:
+                    column = COLUMNS.index(sides[:2]) if any(sides[:2]) else len(COLUMNS)
+                    rows.append(near_labels[column, spot(sides[2], step_row, block_size(sum(subset))), :])
+                return jnp.concatenate(rows, axis=0)
+
+            def gap_rows(subset):
+                if not any(subset):
+                    return own_b[spot(0, own_row, own_row), :]
+                size = block_size(sum(subset))
+                return jnp.concatenate([near_block(s)[spot(s[2], size, size), :] for s in SIDES[subset]], axis=0)
+
+            def product(right):
+                return jnp.dot(turned[phase][e], right.astype(jnp.bfloat16), preferred_element_type=jnp.float32)
+
+            own = current[step, pl.ds(e, 1), :]
+            if step == 0:
+                found = product(diagonal(gap_rows(subsets[0]), gap_rows(subsets[1])))
+                gap[e, phase] = found
+            else:
+                found = gap[e, phase]
+            second = label_rows(subsets[1])
+            if phase == 0:
+                values = product(jnp.concatenate([jnp.zeros((own_row, slots), jnp.float32), second], axis=0))
+                least = jnp.minimum(jnp.maximum(found[:, :slots], own), jnp.maximum(found[:, slots:], values))
+            else:
+                values = product(diagonal(label_rows(subsets[0]), second))
+                either = jnp.maximum(found, values)
+                least = jnp.minimum(lowest[e], jnp.minimum(either[:, :slots], either[:, slots:]))
+            if not last:
+                lowest[e] = least
+                return
+            row = jnp.minimum(jnp.min(least.T, axis=0, keepdims=True), own)
+            filled = slot < counts_ref[e]
+            if step == ITERS - 1:
+                groups_ref[pl.ds(e, 1), :] = jnp.where(filled, row, -1.0).astype(jnp.int32)
+            else:
+                current[step + 1, pl.ds(e, 1), :] = jnp.where(filled, row, sentinel)
 
     for step in range(ITERS):
         if step > 0:
@@ -224,57 +276,18 @@
             for copy in copies:
                 copy.start()
         put_labels(len(COLUMNS), current[step])
-        for copy in copies:
-            copy.wait_recv()
-        for n in range(len(COLUMNS)):
-            put_labels(n, halo_labels[step, n])
-
-        @pl.loop(0, depth, unroll=2)
-        def _(e):
-            cells = {0: e, 1: lax.rem(e + 1, depth), -1: lax.rem(e + depth - 1, depth)}
-
-            def spot(side, stride, size):
-                return pl.ds(pl.multiple_of(cells[side] * stride, size), size)
-
-            own = current[step, pl.ds(e, 1), :]
-            if step == 0:
-                at = pl.multiple_of(e * own_row, 8)
-                found = jnp.dot(
-                    turned0[e],
-                    own_b[pl.ds(at, own_row), :].astype(jnp.bfloat16),
-                    preferred_element_type=jnp.float32,
-                )
-                gap[e, 0] = found
-            else:
-                found = gap[e, 0]
-            least = jnp.maximum(found, own)
-            for m, subset in enumerate(SUBSETS):
-                sides_list = SIDES[subset]
-                left = turned[sum(subset)][place[subset], e]
-                columns = [COLUMNS.index(s[:2]) if s[:2] != (0, 0) else len(COLUMNS) for s in sides_list]
-                size = block_size(sum(subset))
-                right = jnp.concatenate(
-                    [near_labels[c, spot(s[2], step_row, size), :] for c, s in zip(columns, sides_list)], axis=0
-                )
+        for phase, (subsets, columns) in enumerate(PHASES):
+            for n in columns:
                 if step == 0:
-                    front = jnp.concatenate(
-                        [near_block(s)[spot(s[2], size, size), :] for s in sides_list], axis=0
-                    )
-                    both = jnp.concatenate([front, right], axis=1).astype(jnp.bfloat16)
-                    result = jnp.dot(left, both, preferred_element_type=jnp.float32)
-                    found, values = result[:, :slots], result[:, slots:]
-                    gap[e, m + 1] = found
-                else:
-                    values = jnp.dot(left, right.astype(jnp.bfloat16), preferred_element_type=jnp.float32)
-                    found = gap[e, m + 1]
-                least = jnp.minimum(least, jnp.maximum(found, values))
-            row = jnp.minimum(jnp.min(least.T, axis=0, keepdims=True), own)
-            filled = slot < counts_ref[e]
-            if step == ITERS - 1:
-                groups_ref[pl.ds(e, 1), :] = jnp.where(filled, row, -1.0).astype(jnp.int32)
-            else:
-                current[step + 1, pl.ds(e, 1), :] = jnp.where(filled, row, sentinel)
-
+                    point_copies[n].wait_recv()
+                    points = [halo_points[n, k] for k in range(3)]
+                    for sides in BLOCKS:
+                        if sides[:2] == COLUMNS[n]:
+                            size = block_size(sum(abs(side) for side in sides))
+                            put_rows(near_block(sides), near_rows(points, sides), depth, size)
+                copies[n].wait_recv()
+                put_labels(n, halo_labels[step, n])
+            sweep(step, phase, subsets)
         for copy in copies:
             copy.wait_send()
     for copy in point_copies:
@@ -304,11 +317,12 @@
             pltpu.VMEM((len(BLOCKS) - 8, depth * step_row, slots), jnp.float32),
             pltpu.VMEM((8, depth * 8, slots), jnp.float32),
             pltpu.VMEM((near + 1, depth * step_row, slots), jnp.float32),
-            pltpu.VMEM((depth, slots, own_row), jnp.bfloat16),
-            pltpu.VMEM((3, depth, slots, 2 * step_row), jnp.bfloat16),
-            pltpu.VMEM((3, depth, slots, 4 * step_row), jnp.bfloat16),
-            pltpu.VMEM((1, depth, slots, 8 * 8), jnp.bfloat16),
-            pltpu.VMEM((depth, len(SUBSETS) + 1, slots, slots), jnp.float32),
+            pltpu.VMEM((depth, slots, own_row + 2 * step_row), jnp.bfloat16),
+            pltpu.VMEM((depth, slots, 6 * step_row), jnp.bfloat16),
+            pltpu.VMEM((depth, slots, 6 * step_row), jnp.bfloat16),
+            pltpu.VMEM((depth, slots, 8 * step_row), jnp.bfloat16),
+            pltpu.VMEM((depth, len(PHASES), slots, 2 * slots), jnp.float32),
+            pltpu.VMEM((depth, slots, slots), jnp.float32),
             pltpu.SemaphoreType.DMA((near,)),
             pltpu.SemaphoreType.DMA((near,)),
             pltpu.SemaphoreType.DMA((ITERS, near)),

time: 49.9 us -> 44.2 us (0.89)
  the two profiles are of different devices: /device:TPU:1 before, /device:TPU:0 now
where the time goes in v2:
time: 44.2 us; the launch traced here: 43.9 us
  Pallas kernels  42.6 us (96%)
  local copies, waits for them, and re-layouts  1.32 us (3%)
    pallas_call x1, Pallas kernels, body(): pl.pallas_call(kernel, out_shape=jax.ShapeDtypeStruct((depth, slots), jnp...  42.6 us
    unnamed x1, local copies, waits for them, and re-layouts  1.32 us

profile of v2, /device:TPU:0, one launch (start us, length us, event | category | flops | bytes accessed | tf_op | source)
XLA Modules:
  0.0 43.9 jit_solution(16382465674289039913)
XLA Ops:
  0.0 42.6 %shard_map.37 = s32[32,128]{1,0:T(8,128)} custom-call(s32[32]{0:T(128)} %bitcast.7, f32[3,32,128]{2,1,0:T(8,128)} %bitcast.5, s32[32,128]{1,0:T(8,128)} %bitcast.6), custom_call_target="tpu_custom_call" | custom-call | tf_op jit(solution)/shard_map/pallas_call | solution.py:300
  42.6 1.3 %copy.5 = s32[1,1,32,128]{3,2,1,0:T(8,128)} copy(s32[1,1,32,128]{3,2,1,0:T(8,128)} %bitcast.4) | data formatting | bytes 32768

commit v3 on v2

--- a/solution.py
+++ b/solution.py
@@ -15,6 +15,7 @@
 middle = 512.0
 reach = 64.0
 step_row = 16
+head_row = 8
 own_row = 32
 
 MESH = pl.DeviceIdType.MESH
@@ -187,17 +188,23 @@
 
     turned = (turned0, turned1, turned2, turned3)
 
-    @pl.loop(0, depth, unroll=2)
+    @pl.loop(0, depth, unroll=4)
     def _(e):
         for phase, (subsets, _) in enumerate(PHASES):
-            rows = []
+            heads, tails = [], []
             for subset in subsets:
                 if not any(subset):
-                    rows.append(own_a[pl.ds(pl.multiple_of(e * own_row, own_row), own_row), :] * sentinel)
                     continue
                 size = block_size(sum(subset))
                 base = side_a[SUBSETS.index(subset), pl.ds(pl.multiple_of(e * size, size), size), :]
-                rows += [base * hot[BLOCKS.index(sides), pl.ds(e, 1), :] for sides in SIDES[subset]]
+                for sides in SIDES[subset]:
+                    chosen = hot[BLOCKS.index(sides), pl.ds(e, 1), :]
+                    heads.append(base[:head_row] * chosen)
+                    if size > head_row:
+                        tails.append(base[head_row:] * chosen)
+            if phase == 0:
+                tails.append(own_a[pl.ds(pl.multiple_of(e * own_row, own_row), own_row), :] * sentinel)
+            rows = heads + tails
             turned[phase][e] = jnp.concatenate(rows, axis=0).T.astype(jnp.bfloat16)
 
     like = own_points[0]
@@ -211,19 +218,18 @@
 
     def put_labels(n, value):
         for k, row in enumerate(thirds(value)):
-            near_labels[n, pl.ds(k, depth, stride=step_row), :] = row * (1.0 / sentinel)
+            near_labels[n, pl.ds(k, depth, stride=head_row), :] = row * (1.0 / sentinel)
 
     near_labels[...] = jnp.zeros_like(near_labels)
 
-    def diagonal(first, second):
-        top = jnp.concatenate([first, jnp.zeros((first.shape[0], second.shape[1]), first.dtype)], axis=1)
-        low = jnp.concatenate([jnp.zeros((second.shape[0], first.shape[1]), first.dtype), second], axis=1)
-        return jnp.concatenate([top, low], axis=0)
+    def wide(block, half):
+        blank = jnp.zeros_like(block)
+        return jnp.concatenate([blank, block] if half else [block, blank], axis=1)
 
     def sweep(step, phase, subsets):
         last = phase == len(PHASES) - 1
 
-        @pl.loop(0, depth, unroll=4)
+        @pl.loop(0, depth, unroll=8)
         def _(e):
             cells = {0: e, 1: lax.rem(e + 1, depth), -1: lax.rem(e + depth - 1, depth)}
 
@@ -234,30 +240,43 @@
                 rows = []
                 for sides in SIDES[subset]:
                     column = COLUMNS.index(sides[:2]) if any(sides[:2]) else len(COLUMNS)
-                    rows.append(near_labels[column, spot(sides[2], step_row, block_size(sum(subset))), :])
+                    rows.append(near_labels[column, spot(sides[2], head_row, head_row), :])
                 return jnp.concatenate(rows, axis=0)
 
-            def gap_rows(subset):
-                if not any(subset):
-                    return own_b[spot(0, own_row, own_row), :]
-                size = block_size(sum(subset))
-                return jnp.concatenate([near_block(s)[spot(s[2], size, size), :] for s in SIDES[subset]], axis=0)
+            def gap_rows():
+                heads, tails = [], []
+                for half, subset in enumerate(subsets):
+                    if not any(subset):
+                        continue
+                    size = block_size(sum(subset))
+                    for sides in SIDES[subset]:
+                        block = near_block(sides)[spot(sides[2], size, size), :]
+                        heads.append(wide(block[:head_row], half))
+                        if size > head_row:
+                            tails.append(wide(block[head_row:], half))
+                if phase == 0:
+                    tails.append(wide(own_b[spot(0, own_row, own_row), :], 0))
+                return jnp.concatenate(heads + tails, axis=0)
+
+            left = turned[phase][e]
 
             def product(right):
-                return jnp.dot(turned[phase][e], right.astype(jnp.bfloat16), preferred_element_type=jnp.float32)
+                return jnp.dot(
+                    left[:, : right.shape[0]], right.astype(jnp.bfloat16), preferred_element_type=jnp.float32
+                )
 
             own = current[step, pl.ds(e, 1), :]
             if step == 0:
-                found = product(diagonal(gap_rows(subsets[0]), gap_rows(subsets[1])))
+                found = product(gap_rows())
                 gap[e, phase] = found
             else:
                 found = gap[e, phase]
             second = label_rows(subsets[1])
             if phase == 0:
-                values = product(jnp.concatenate([jnp.zeros((own_row, slots), jnp.float32), second], axis=0))
+                values = product(second)
                 least = jnp.minimum(jnp.maximum(found[:, :slots], own), jnp.maximum(found[:, slots:], values))
             else:
-                values = product(diagonal(label_rows(subsets[0]), second))
+                values = product(jnp.concatenate([wide(label_rows(subsets[0]), 0), wide(second, 1)], axis=0))
                 either = jnp.maximum(found, values)
                 least = jnp.minimum(lowest[e], jnp.minimum(either[:, :slots], either[:, slots:]))
             if not last:
@@ -316,7 +335,7 @@
             pltpu.VMEM((len(BLOCKS), depth, slots), jnp.float32),
             pltpu.VMEM((len(BLOCKS) - 8, depth * step_row, slots), jnp.float32),
             pltpu.VMEM((8, depth * 8, slots), jnp.float32),
-            pltpu.VMEM((near + 1, depth * step_row, slots), jnp.float32),
+            pltpu.VMEM((near + 1, depth * head_row, slots), jnp.float32),
             pltpu.VMEM((depth, slots, own_row + 2 * step_row), jnp.bfloat16),
             pltpu.VMEM((depth, slots, 6 * step_row), jnp.bfloat16),
             pltpu.VMEM((depth, slots, 6 * step_row), jnp.bfloat16),

time: 44.2 us -> 36.7 us (0.83)
  Pallas kernels: 42.6 us -> 35.1 us
    pallas_call x1, Pallas kernels: 42.6 us -> 35.1 us  [body(): pl.pallas_call(kernel, out_shape=jax.ShapeDtypeStruct((depth, slots), jnp...]
where the time goes in v3:
time: 36.7 us; the launch traced here: 36.4 us
  Pallas kernels  35.1 us (96%)
  local copies, waits for them, and re-layouts  1.32 us (4%)
    pallas_call x1, Pallas kernels, body(): pl.pallas_call(kernel, out_shape=jax.ShapeDtypeStruct((depth, slots), jnp...  35.1 us
    unnamed x1, local copies, waits for them, and re-layouts  1.32 us

profile of v3, /device:TPU:0, one launch (start us, length us, event | category | flops | bytes accessed | tf_op | source)
XLA Modules:
  0.0 36.4 jit_solution(13196800796232984324)
XLA Ops:
  0.0 35.1 %shard_map.37 = s32[32,128]{1,0:T(8,128)} custom-call(s32[32]{0:T(128)} %bitcast.7, f32[3,32,128]{2,1,0:T(8,128)} %bitcast.5, s32[32,128]{1,0:T(8,128)} %bitcast.6), custom_call_target="tpu_custom_call" | custom-call | tf_op jit(solution)/shard_map/pallas_call | solution.py:319
  35.1 1.3 %copy.5 = s32[1,1,32,128]{3,2,1,0:T(8,128)} copy(s32[1,1,32,128]{3,2,1,0:T(8,128)} %bitcast.4) | data formatting | bytes 32768

commit v4 on v3

--- a/solution.py
+++ b/solution.py
@@ -136,8 +136,6 @@
         here = labels_ref[e : e + 1, :].astype(jnp.float32)
         current[0, e : e + 1, :] = jnp.where(slot < counts_ref[e], here, sentinel)
 
-    pl.semaphore_wait(barrier, len(COLUMNS))
-
     def label_copies(step):
         return [
             pltpu.make_async_remote_copy(
@@ -162,11 +160,6 @@
         )
         for n, offset in enumerate(COLUMNS)
     ]
-    copies = label_copies(0)
-    for point_copy, label_copy in zip(point_copies, copies):
-        point_copy.start()
-        label_copy.start()
-
     own_points = [points_ref[k] for k in range(3)]
 
     def near_block(sides):
@@ -185,6 +178,12 @@
                 here = high if side > 0 else jnp.logical_not(high)
                 chosen = here if chosen is None else jnp.logical_and(chosen, here)
         hot[n] = jnp.where(chosen, sentinel, 0.0)
+
+    pl.semaphore_wait(barrier, len(COLUMNS))
+    copies = label_copies(0)
+    for point_copy, label_copy in zip(point_copies, copies):
+        point_copy.start()
+        label_copy.start()
 
     turned = (turned0, turned1, turned2, turned3)
 
@@ -205,7 +204,7 @@
             if phase == 0:
                 tails.append(own_a[pl.ds(pl.multiple_of(e * own_row, own_row), own_row), :] * sentinel)
             rows = heads + tails
-            turned[phase][e] = jnp.concatenate(rows, axis=0).T.astype(jnp.bfloat16)
+            turned[phase][e] = jnp.concatenate(rows, axis=0).astype(jnp.bfloat16).T
 
     like = own_points[0]
     put_rows(own_b, fixed_rows((0, 0, 0), own_row, like), depth, own_row)
@@ -229,7 +228,7 @@
     def sweep(step, phase, subsets):
         last = phase == len(PHASES) - 1
 
-        @pl.loop(0, depth, unroll=8)
+        @pl.loop(0, depth, unroll=16)
         def _(e):
             cells = {0: e, 1: lax.rem(e + 1, depth), -1: lax.rem(e + depth - 1, depth)}
 

time: 36.7 us -> 34.5 us (0.940)
  Pallas kernels: 35.1 us -> 32.8 us
    pallas_call x1, Pallas kernels: 35.1 us -> 32.8 us  [body(): pl.pallas_call(kernel, out_shape=jax.ShapeDtypeStruct((depth, slots), jnp...]
where the time goes in v4:
time: 34.5 us; the launch traced here: 34.2 us
  Pallas kernels  32.8 us (95%)
  local copies, waits for them, and re-layouts  1.32 us (4%)
    pallas_call x1, Pallas kernels, body(): pl.pallas_call(kernel, out_shape=jax.ShapeDtypeStruct((depth, slots), jnp...  32.8 us
    unnamed x1, local copies, waits for them, and re-layouts  1.32 us

profile of v4, /device:TPU:0, one launch (start us, length us, event | category | flops | bytes accessed | tf_op | source)
XLA Modules:
  0.0 34.2 jit_solution(17221054447733219291)
XLA Ops:
  0.0 32.8 %shard_map.37 = s32[32,128]{1,0:T(8,128)} custom-call(s32[32]{0:T(128)} %bitcast.7, f32[3,32,128]{2,1,0:T(8,128)} %bitcast.5, s32[32,128]{1,0:T(8,128)} %bitcast.6), custom_call_target="tpu_custom_call" | custom-call | tf_op jit(solution)/shard_map/pallas_call | solution.py:318
  32.9 1.3 %copy.5 = s32[1,1,32,128]{3,2,1,0:T(8,128)} copy(s32[1,1,32,128]{3,2,1,0:T(8,128)} %bitcast.4) | data formatting | bytes 32768

commit v5 on v4

--- a/solution.py
+++ b/solution.py
@@ -151,11 +151,11 @@
 
     point_copies = [
         pltpu.make_async_remote_copy(
-            src_ref=points_ref,
+            src_ref=halo_points.at[COLUMNS.index((0, offset[1]))] if all(offset) else points_ref,
             dst_ref=halo_points.at[n],
             send_sem=point_send.at[n],
             recv_sem=point_recv.at[n],
-            device_id=target(offset),
+            device_id=target((offset[0], 0) if all(offset) else offset),
             device_id_type=MESH,
         )
         for n, offset in enumerate(COLUMNS)
@@ -181,8 +181,9 @@
 
     pl.semaphore_wait(barrier, len(COLUMNS))
     copies = label_copies(0)
-    for point_copy, label_copy in zip(point_copies, copies):
-        point_copy.start()
+    for n, label_copy in enumerate(copies):
+        if not all(COLUMNS[n]):
+            point_copies[n].start()
         label_copy.start()
 
     turned = (turned0, turned1, turned2, turned3)
@@ -288,6 +289,11 @@
             else:
                 current[step + 1, pl.ds(e, 1), :] = jnp.where(filled, row, sentinel)
 
+    for n in (2, 3):
+        point_copies[n].wait_recv()
+    for n in (4, 5, 6, 7):
+        point_copies[n].start()
+
     for step in range(ITERS):
         if step > 0:
             copies = label_copies(step)
@@ -297,7 +303,8 @@
         for phase, (subsets, columns) in enumerate(PHASES):
             for n in columns:
                 if step == 0:
-                    point_copies[n].wait_recv()
+                    if n not in (2, 3):
+                        point_copies[n].wait_recv()
                     points = [halo_points[n, k] for k in range(3)]
                     for sides in BLOCKS:
                         if sides[:2] == COLUMNS[n]:

time: 34.5 us -> 34.2 us (level)
  no operation moved by 1% of the time
where the time goes in v5:
time: 34.2 us; the launch traced here: 33.9 us
  Pallas kernels  32.6 us (95%)
  local copies, waits for them, and re-layouts  1.32 us (4%)
    pallas_call x1, Pallas kernels, body(): pl.pallas_call(kernel, out_shape=jax.ShapeDtypeStruct((depth, slots), jnp...  32.6 us
    unnamed x1, local copies, waits for them, and re-layouts  1.32 us

profile of v5, /device:TPU:0, one launch (start us, length us, event | category | flops | bytes accessed | tf_op | source)
XLA Modules:
  0.0 33.9 jit_solution(17218299893326294342)
XLA Ops:
  0.0 32.6 %shard_map.37 = s32[32,128]{1,0:T(8,128)} custom-call(s32[32]{0:T(128)} %bitcast.7, f32[3,32,128]{2,1,0:T(8,128)} %bitcast.5, s32[32,128]{1,0:T(8,128)} %bitcast.6), custom_call_target="tpu_custom_call" | custom-call | tf_op jit(solution)/shard_map/pallas_call | solution.py:325
  32.6 1.3 %copy.5 = s32[1,1,32,128]{3,2,1,0:T(8,128)} copy(s32[1,1,32,128]{3,2,1,0:T(8,128)} %bitcast.4) | data formatting | bytes 32768
